TPU v7x, 256 devices: a whole 4x4x8 slice. The times are simulated.
256 devices in a mesh: rep: 32 (over z, y), tp: 8 (over x, core).
Axes of the slice: x: 4, y: 4, z: 8, core: 2. Of those that a mesh axis runs over, the one named last changes fastest.
Arguments:
- image_grads: bfloat16 [512, 48, 1280], P('rep', 'tp'), may hold values from -6 to 6
- dest_rank: int32 [512], P('rep'), may hold values from 0 to 31, as said below
- dest_slot: int32 [512], P('rep'), may hold values from 0 to 31, as said below
- saved_inputs: bfloat16 [1024, 48, 1280], P('rep'), may hold values from -6 to 6
- up_weight: bfloat16 [1280, 5120], P(None, 'tp'), may hold values from -0.15625 to 0.15625
- down_weight: bfloat16 [5120, 1280], P('tp'), may hold values from -0.078125 to 0.078125
- norm_gain: float32 [1280], replicated, may hold values from 0.25 to 1.75
Outputs:
- input_grads: bfloat16 [1024, 48, 1280], P('rep', 'tp')
- up_grads: float32 [1280, 5120], P('rep', 'tp')
- down_grads: float32 [5120, 1280], P('tp', 'rep')
- gain_grads: float32 [1280], replicated
Inputs may be any that keep to these rules, and one draw needn't show every extreme that they name: `dest_rank`: the images of one index of rep go to different owners; each owner receives at most 32 images, and some owner receives exactly 32 in every draw. `dest_slot`: the images that one owner receives have distinct slots 0, 1, ... up to their count less one; other slots hold no image.
All inputs are finite; a program needn't handle non-finite values.
Results may differ from a plain program's by a relative error of at most 0.015.
Values may be sent and summed in bfloat16 or wider, within the bound.
A program may use at most 128 MiB of HBM per device.

v0:
```python
import jax
import jax.numpy as jnp
from jax import lax
from jax.sharding import Mesh
from jax.sharding import PartitionSpec as P

REP = ("rep_0", "rep_1")


epsilon = 1e-05
gelu_c = 0.7978845608028654
gelu_a = 0.044715


def scatter_axes(value, axes, dim):
    if not axes:
        return value
    nearer = lax.psum_scatter(value, axes[0], scatter_dimension=dim, tiled=True)
    return scatter_axes(nearer, axes[1:], dim)


def sent_to_all(value, axis):
    copies = jnp.broadcast_to(value, (lax.axis_size(axis), *value.shape))
    return lax.all_to_all(copies, axis, split_axis=0, concat_axis=0, tiled=True)


def of_everyone(value, axis):
    everything = sent_to_all(value, axis)
    return jnp.sum(everything, axis=0)


def gelu_value(preact):
    inner = jnp.tanh(gelu_c * (preact + gelu_a * preact**3))
    return 0.5 * preact * (1.0 + inner)


def gelu_slope(preact):
    inner = jnp.tanh(gelu_c * (preact + gelu_a * preact**3))
    return 0.5 * (1.0 + inner) + 0.5 * preact * (1.0 - inner * inner) * gelu_c * (
        1.0 + 3.0 * gelu_a * preact * preact
    )


def outbound(images, dest_rank, dest_slot, groups, capacity):
    rank_ids = jnp.arange(groups, dtype=jnp.int32)
    one_hot = dest_rank[None, :] == rank_ids[:, None]
    packed = jnp.einsum(
        "ek,kpd->epd", one_hot.astype(jnp.bfloat16), images, preferred_element_type=jnp.float32
    ).astype(jnp.bfloat16)
    present = jnp.any(one_hot, axis=1)
    slot_sent = jnp.sum(jnp.where(one_hot, dest_slot[None, :], 0), axis=1) + jnp.where(
        present, 0, capacity
    )
    return (packed, slot_sent)


def compact(inbound, slot_recv, capacity):
    slot_ids = jnp.arange(capacity, dtype=jnp.int32)
    picker = (slot_recv[None, :] == slot_ids[:, None]).astype(jnp.bfloat16)
    return jnp.einsum("ce,epd->cpd", picker, inbound, preferred_element_type=jnp.float32).astype(
        jnp.bfloat16
    )


def local(image_grads, dest_rank, dest_slot, saved_inputs, up_weight, down_weight, norm_gain):
    groups = lax.axis_size(REP)
    capacity = saved_inputs.shape[0]
    patches = saved_inputs.shape[1]
    width = saved_inputs.shape[2]
    slab = image_grads.shape[1]
    packed, slot_sent = outbound(image_grads, dest_rank, dest_slot, groups, capacity)
    inbound, slot_recv = (
        lax.all_to_all(packed, REP, split_axis=0, concat_axis=0, tiled=True),
        lax.all_to_all(slot_sent, REP, split_axis=0, concat_axis=0, tiled=True),
    )
    routed = lax.all_gather(compact(inbound, slot_recv, capacity), "tp", axis=1, tiled=True)
    rows = capacity * patches
    grads = routed.reshape(rows, width)
    values = saved_inputs.reshape(rows, width).astype(jnp.float32)
    mean_v = jnp.mean(values, axis=1, keepdims=True)
    var_v = jnp.mean((values - mean_v) ** 2, axis=1, keepdims=True)
    inv_std = 1.0 / jnp.sqrt(var_v + epsilon)
    centred = (values - mean_v) * inv_std
    normed = (centred * norm_gain[None, :]).astype(jnp.bfloat16)
    preact = jnp.dot(normed, up_weight, preferred_element_type=jnp.float32)
    hidden = gelu_value(preact).astype(jnp.bfloat16)
    grad_hidden = jnp.dot(grads, down_weight.T, preferred_element_type=jnp.float32)
    grad_pre = (grad_hidden * gelu_slope(preact)).astype(jnp.bfloat16)
    down_local = jnp.dot(hidden.T, grads, preferred_element_type=jnp.float32)
    up_local = jnp.dot(normed.T, grad_pre, preferred_element_type=jnp.float32)
    partial_normed = jnp.dot(grad_pre, up_weight.T, preferred_element_type=jnp.float32)
    up_grads, down_grads = (
        scatter_axes(up_local.astype(jnp.bfloat16), REP, 0).astype(jnp.float32),
        scatter_axes(down_local.astype(jnp.bfloat16), REP, 1).astype(jnp.float32),
    )
    start = lax.axis_index("tp") * slab
    grad_normed = lax.psum(partial_normed.astype(jnp.bfloat16), "tp").astype(jnp.float32)
    gain_grads = of_everyone(jnp.sum(grad_normed * centred, axis=0), REP)
    scaled = grad_normed * norm_gain[None, :]
    first = jnp.mean(scaled, axis=1, keepdims=True)
    second = jnp.mean(scaled * centred, axis=1, keepdims=True)
    result = grads.astype(jnp.float32) + inv_std * (scaled - first - centred * second)
    result = result.reshape(capacity, patches, width)
    input_grads = lax.dynamic_slice_in_dim(result, start, slab, 1).astype(jnp.bfloat16)
    return (input_grads, up_grads, down_grads, gain_grads)


def solution(mesh):
    split = Mesh(mesh.devices.reshape(8, 4, mesh.shape["tp"]), ("rep_0", "rep_1", "tp"))
    return jax.shard_map(
        local,
        mesh=split,
        in_specs=(
            P(REP, "tp", None),
            P(REP),
            P(REP),
            P(REP, None, None),
            P(None, "tp"),
            P("tp", None),
            P(),
        ),
        out_specs=(P(REP, "tp", None), P(REP, "tp"), P("tp", REP), P()),
        check_vma=False,
    )
```

profile of v0, /device:TPU:2, one launch (start us, length us, event | category | flops | bytes accessed | tf_op | source)
XLA Modules:
  0.0 318.9 jit_solution(2042661000471552826)
XLA Ops:
  7.2 0.0 copy-start
  7.2 0.9 fusion.27
  8.0 0.8 select_reduce_fusion
  8.8 0.7 copy.29
  9.5 11.5 %all-to-all-start = ((s32[32,1,1]{2,1,0:T(1,128)}), s32[32,1,1]{2,1,0:T(1,128)S(1)}, u32[]{:S(2)}, u32[]{:S(2)}) async-start(s32[32,1,1]{2,1,0:T(1,128)} %copy.29), calls=%async_computation | async-start | bytes 32768 | tf_op jit(solution)/shard_map/all_to_all | solution.py:74
  21.0 1.4 convolution_convert_fusion.4
  22.4 1.1 copy.30
  23.5 7.2 %all-to-all-done = s32[32,1,1]{2,1,0:T(1,128)S(1)} async-done(((s32[32,1,1]{2,1,0:T(1,128)}), s32[32,1,1]{2,1,0:T(1,128)S(1)}, u32[]{:S(2)}, u32[]{:S(2)}) %all-to-all-start) | async-done | bytes 160 | tf_op jit(solution)/shard_map/all_to_all | solution.py:74
  30.7 3.9 %all-to-all-start.1 = ((bf16[32,6,1280]{2,1,0:T(8,128)(2,1)}), bf16[32,6,1280]{2,1,0:T(8,128)(2,1)S(1)}, u32[]{:S(2)}, u32[]{:S(2)}) async-start(bf16[32,6,1280]{2,1,0:T(8,128)(2,1)} %copy.30), calls=%async_computation.1 | async-start | bytes 1310720 | tf_op jit(solution)/shard_map/all_to_all | solution.py:73
  34.6 0.0 all-gather.2.cloned.1.call-start
  34.6 0.7 reduce.3
  35.3 18.5 %all-to-all-done.1 = bf16[32,6,1280]{2,1,0:T(8,128)(2,1)S(1)} async-done(((bf16[32,6,1280]{2,1,0:T(8,128)(2,1)}), bf16[32,6,1280]{2,1,0:T(8,128)(2,1)S(1)}, u32[]{:S(2)}, u32[]{:S(2)}) %all-to-all-start.1) | async-done | bytes 491552 | tf_op jit(solution)/shard_map/all_to_all | solution.py:73
  53.8 1.1 convolution_convert_fusion.3
  54.8 0.0 all-gather.2.cloned.1.call-update
  54.8 0.0 copy-start.3
  54.9 0.2 reduce-scatter.11.cloned.1.call-start
  55.1 2.7 convert_reduce_fusion
  57.8 0.1 div.18
  57.9 3.3 %multiply_reduce_fusion = f32[32,48]{1,0:T(8,128)S(1)} fusion(bf16[32,48,1280]{2,1,0:T(8,128)(2,1)} %param.10, f32[32,48]{1,0:T(8,128)S(1)} %broadcast_multiply_fusion), kind=kLoop, calls=%fused_computation.13 | loop fusion | flops 7862784 | bytes 3944448 | tf_op jit(solution)/shard_map/reduce_sum | solution.py:81
  61.2 0.1 sqrt.6
  61.3 0.0 copy-done.3
  61.3 3.0 multiply_convert_fusion
  64.3 0.0 copy-start.2
  64.3 2.0 copy-done.2
  66.3 0.0 copy-done
  66.3 5.2 %fusion.34 = f32[1536,640]{1,0:T(8,128)} fusion(bf16[1536,1280]{1,0:T(8,128)(2,1)S(1)} %multiply_convert_fusion, bf16[1280,640]{1,0:T(8,128)(2,1)S(1)} %copy-done), kind=kOutput, calls=%fused_computation.56 | convolution fusion | flops 2516582400 | bytes 9502720 | tf_op jit(solution)/shard_map/dot_general | solution.py:85
  71.5 12.3 %all-gather.2.cloned.1.call-done = bf16[32,48,1280]{2,0,1:T(8,128)(2,1)} async-done(((bf16[32,6,1280]{2,0,1:T(8,128)(2,1)}), bf16[32,48,1280]{2,0,1:T(8,128)(2,1)}) %all-gather.2.cloned.1.call-update) | async-done | bytes 3932176 | tf_op jit(solution)/shard_map/all_gather | solution.py:76
  83.8 0.0 copy-start.5
  83.8 4.4 %copy.32 = bf16[32,48,1280]{2,1,0:T(8,128)(2,1)S(1)} copy(bf16[32,48,1280]{2,0,1:T(8,128)(2,1)} %all-gather.2.cloned.1.call-done) | data formatting | bytes 7864320 | tf_op jit(solution)/shard_map/all_gather | solution.py:76
  88.2 0.0 copy-start.1
  88.2 1.9 copy-done.1
  90.1 0.0 copy-done.5
  90.1 0.0 copy-start.4
  90.1 5.1 %convolution_convert_fusion.1 = bf16[640,1280]{0,1:T(8,128)(2,1)} fusion(bf16[1536,1280]{1,0:T(8,128)(2,1)S(1)} %bitcast.34, f32[1536,640]{1,0:T(8,128)S(1)} %copy-done.5), kind=kOutput, calls=%fused_computation.28 | convolution fusion | flops 2526248960 | bytes 9502720 | tf_op jit(solution)/shard_map/dot_general | solution.py:89
  95.2 0.0 reduce-scatter.11.cloned.1.call-update
  95.2 0.3 all-reduce.4.cloned.1.call-start
  95.5 0.0 copy-done.4
  95.5 8.2 %fusion.17 = bf16[1536,640]{1,0:T(8,128)(2,1)S(1)} fusion(f32[1536,640]{1,0:T(8,128)} %fusion.34, bf16[1536,1280]{1,0:T(8,128)(2,1)} %bitcast.35, bf16[640,1280]{1,0:T(8,128)(2,1)S(1)} %copy-done.4), kind=kOutput, calls=%fused_computation.26 | convolution fusion | flops 2535260160 | bytes 11468800 | tf_op jit(solution)/shard_map/dot_general | solution.py:87
  103.7 0.0 copy-start.6
  103.7 1.3 copy-done.6
  104.9 4.7 %convolution_convert_fusion = bf16[1536,1280]{1,0:T(8,128)(2,1)} fusion(bf16[1536,640]{1,0:T(8,128)(2,1)S(1)} %fusion.17, bf16[1280,640]{1,0:T(8,128)(2,1)S(1)} %copy-done), kind=kOutput, calls=%fused_computation.14 | convolution fusion | flops 2518548480 | bytes 7536640 | tf_op jit(solution)/shard_map/dot_general | solution.py:91
  109.7 0.0 all-reduce.4.cloned.1.call-update
  109.7 0.0 reduce-scatter.9.cloned.1.call-start
  109.7 7.2 %convolution_convert_fusion.2 = bf16[1280,640]{1,0:T(8,128)(2,1)} fusion(bf16[1536,1280]{1,0:T(8,128)(2,1)} %copy-done.2, bf16[1536,640]{1,0:T(8,128)(2,1)} %copy-done.6), kind=kOutput, calls=%fused_computation.29 | convolution fusion | flops 2517401600 | bytes 7536640 | tf_op jit(solution)/shard_map/dot_general | solution.py:90
  116.9 0.0 reduce-scatter.9.cloned.1.call-update
  116.9 0.0 reduce-scatter.15.cloned.1.call-start
  117.0 20.4 %reduce-scatter.11.cloned.1.call-done = bf16[640,160]{0,1:T(8,128)(2,1)} async-done(((bf16[640,1280]{0,1:T(8,128)(2,1)}), bf16[640,160]{0,1:T(8,128)(2,1)}) %reduce-scatter.11.cloned.1.call-update) | async-done | bytes 204816 | tf_op jit(solution)/shard_map/reduce_scatter | solution.py:18
  137.4 0.0 reduce-scatter.15.cloned.1.call-update
  137.4 74.8 %all-reduce.4.cloned.1.call-done = bf16[1536,1280]{1,0:T(8,128)(2,1)} async-done(((bf16[1536,1280]{1,0:T(8,128)(2,1)}), bf16[1536,1280]{1,0:T(8,128)(2,1)}) %all-reduce.4.cloned.1.call-update) | async-done | bytes 3932176 | tf_op jit(solution)/shard_map/psum | solution.py:97
  212.2 5.8 %fusion.7 = (f32[1280]{0:T(1024)S(1)}, f32[1536]{0:T(1024)S(1)}, f32[1536]{0:T(1024)S(1)}) fusion(bf16[1536,1280]{1,0:T(8,128)(2,1)} %all-reduce.4.cloned.1.call-done, bf16[32,48,1280]{2,1,0:T(8,128)(2,1)} %param.10, f32[1536]{0:T(1024)S(1)} %div.18, f32[1536]{0:T(1024)S(1)} %sqrt.6, f32[1280]{0:T(1024)S(1)} %copy-done.3), kind=kLoop, calls=%fused_computation.9 | loop fusion | flops 19656448 | bytes 7899136 | tf_op jit(solution)/shard_map/reduce_sum | solution.py:98
  218.0 0.7 broadcast_in_dim.38
  218.8 9.9 %all-to-all-start.2 = ((f32[32,1,1280]{2,1,0:T(1,128)}), f32[32,1,1280]{2,1,0:T(1,128)S(1)}, u32[]{:S(2)}, u32[]{:S(2)}) async-start(f32[32,1,1280]{2,1,0:T(1,128)} %broadcast_in_dim.38), calls=%async_computation.4 | async-start | bytes 327680 | tf_op jit(solution)/shard_map/all_to_all | solution.py:24
  228.6 0.0 reduce-scatter.13.cloned.1.call-start
  228.7 31.9 %reduce-scatter.9.cloned.1.call-done = bf16[160,640]{1,0:T(8,128)(2,1)} async-done(((bf16[1280,640]{1,0:T(8,128)(2,1)}), bf16[160,640]{1,0:T(8,128)(2,1)}) %reduce-scatter.9.cloned.1.call-update) | async-done | bytes 204816 | tf_op jit(solution)/shard_map/reduce_scatter | solution.py:18
  260.6 0.0 reduce-scatter.13.cloned.1.call-update
  260.6 6.1 %fusion.5 = bf16[1536,1280]{1,0:T(8,128)(2,1)S(1)} fusion(bf16[1536,1280]{1,0:T(8,128)(2,1)} %all-reduce.4.cloned.1.call-done, bf16[32,48,1280]{2,1,0:T(8,128)(2,1)} %param.10, f32[1536]{0:T(1024)S(1)} %get-tuple-element.7, f32[1536]{0:T(1024)S(1)} %get-tuple-element.8, f32[1280]{0:T(1024)S(1)} %copy-done.3, f32[1536]{0:T(1024)S(1)} %div.18, ...), kind=kLoop, calls=%fused_computation.7 | loop fusion | flops 23592960 | bytes 15758336 | tf_op jit(solution)/shard_map/add | solution.py:102
  266.7 0.2 constant_dynamic-slice_fusion
  266.9 0.9 copy.40
  267.8 0.0 all-to-all-done.2
  267.8 0.7 reduce_sum.69
  268.5 16.8 %reduce-scatter.15.cloned.1.call-done = bf16[640,40]{0,1:T(8,128)(2,1)} async-done(((bf16[640,160]{0,1:T(8,128)(2,1)}), bf16[640,40]{0,1:T(8,128)(2,1)}) %reduce-scatter.15.cloned.1.call-update) | async-done | bytes 51216
  285.3 1.5 convert_element_type.66
  286.8 23.8 %reduce-scatter.13.cloned.1.call-done = bf16[40,640]{1,0:T(8,128)(2,1)} async-done(((bf16[160,640]{1,0:T(8,128)(2,1)}), bf16[40,640]{1,0:T(8,128)(2,1)}) %reduce-scatter.13.cloned.1.call-update) | async-done | bytes 51216
  310.6 1.5 convert_element_type.63
  (4 shorter events, 0.0 us)
Async XLA Ops:
  7.2 59.1 %copy-start = (bf16[1280,640]{1,0:T(8,128)(2,1)S(1)}, bf16[1280,640]{1,0:T(8,128)(2,1)}, u32[]{:S(2)}) copy-start(bf16[1280,640]{1,0:T(8,128)(2,1)} %param.11) | copy-start | bytes 4915204
  9.5 21.2 %all-to-all-start = ((s32[32,1,1]{2,1,0:T(1,128)}), s32[32,1,1]{2,1,0:T(1,128)S(1)}, u32[]{:S(2)}, u32[]{:S(2)}) async-start(s32[32,1,1]{2,1,0:T(1,128)} %copy.29), calls=%async_computation | async-start | bytes 32768 | tf_op jit(solution)/shard_map/all_to_all | solution.py:74
  30.7 23.1 %all-to-all-start.1 = ((bf16[32,6,1280]{2,1,0:T(8,128)(2,1)}), bf16[32,6,1280]{2,1,0:T(8,128)(2,1)S(1)}, u32[]{:S(2)}, u32[]{:S(2)}) async-start(bf16[32,6,1280]{2,1,0:T(8,128)(2,1)} %copy.30), calls=%async_computation.1 | async-start | bytes 1310720 | tf_op jit(solution)/shard_map/all_to_all | solution.py:73
  34.6 49.2 %all-gather.2.cloned.1.call-start = ((), (), s32[]{:S(2)}) async-start(), calls=%async_computation.7 | async-start | bytes 4423680 | tf_op jit(solution)/shard_map/all_gather | solution.py:76
  54.8 6.4 %copy-start.3 = (f32[1280]{0:T(1024)S(1)}, f32[1280]{0:T(1024)}, u32[]{:S(2)}) copy-start(f32[1280]{0:T(1024)} %param.13) | copy-start | bytes 15364
  54.9 82.5 %reduce-scatter.11.cloned.1.call-start = ((), (), s32[]{:S(2)}) async-start(), calls=%async_computation.10 | async-start | bytes 1843200 | tf_op jit(solution)/shard_map/reduce_scatter | solution.py:18
  64.3 2.0 copy-start.2
  83.8 6.3 %copy-start.5 = (f32[1536,640]{1,0:T(8,128)S(1)}, f32[1536,640]{1,0:T(8,128)}, u32[]{:S(2)}) copy-start(f32[1536,640]{1,0:T(8,128)} %fusion.34) | copy-start | bytes 11796484
  88.2 1.9 copy-start.1
  90.1 5.4 %copy-start.4 = (bf16[640,1280]{1,0:T(8,128)(2,1)S(1)}, bf16[640,1280]{1,0:T(8,128)(2,1)}, u32[]{:S(2)}) copy-start(bf16[640,1280]{1,0:T(8,128)(2,1)} %param.12) | copy-start | bytes 4915204
  95.2 117.0 %all-reduce.4.cloned.1.call-start = ((), (), s32[]{:S(2)}) async-start(), calls=%async_computation.8 | async-start | bytes 7864320 | tf_op jit(solution)/shard_map/psum | solution.py:97
  103.7 1.3 copy-start.6
  109.7 150.9 %reduce-scatter.9.cloned.1.call-start = ((), (), s32[]{:S(2)}) async-start(), calls=%async_computation.9 | async-start | bytes 1843200 | tf_op jit(solution)/shard_map/reduce_scatter | solution.py:18
  116.9 168.4 %reduce-scatter.15.cloned.1.call-start = ((), (), s32[]{:S(2)}) async-start(), calls=%async_computation.12 | async-start | bytes 256000
  218.8 49.0 %all-to-all-start.2 = ((f32[32,1,1280]{2,1,0:T(1,128)}), f32[32,1,1280]{2,1,0:T(1,128)S(1)}, u32[]{:S(2)}, u32[]{:S(2)}) async-start(f32[32,1,1280]{2,1,0:T(1,128)} %broadcast_in_dim.38), calls=%async_computation.4 | async-start | bytes 327680 | tf_op jit(solution)/shard_map/all_to_all | solution.py:24
  228.6 82.0 %reduce-scatter.13.cloned.1.call-start = ((), (), s32[]{:S(2)}) async-start(), calls=%async_computation.11 | async-start | bytes 256000
Sparse Core Ops, SparseCore 0:
  55.0 28.8 all-gather.1
  95.3 41.9 reduce-scatter.10
  139.7 72.4 all-reduce.3
  214.6 45.9 reduce-scatter.8
  263.0 22.2 reduce-scatter.14
  287.7 22.8 reduce-scatter.12
where the time goes:
time: 319 us
  waiting for transfers between devices  206 us (65%)
  matrix products  32.8 us (10%)
  other arithmetic  26.8 us (8%)
  starting transfers between devices  25.9 us (8%)
  between operations  14.3 us (4%)
  local copies, waits for them, and re-layouts  13.3 us (4%)
    psum x1, waiting for transfers between devices, local(): lax.psum(partial_normed.astype(jnp.bfloat16), 'tp').astype(jnp.float32)  74.8 us
    reduce_scatter x2, waiting for transfers between devices, scatter_axes(): nearer = lax.psum_scatter(value, axes[0], scatter_dimension=dim, tiled=True)  52.3 us
    unnamed x8, waiting for transfers between devices  40.7 us
    all_to_all x1, waiting for transfers between devices, local(): lax.all_to_all(packed, REP, split_axis=0, concat_axis=0, tiled=True)  18.5 us
    all_gather x1, waiting for transfers between devices, local(): lax.all_gather(compact(inbound, slot_recv, capacity), 'tp', axis=1, tiled...  12.3 us
    all_to_all x1, starting transfers between devices, local(): lax.all_to_all(slot_sent, REP, split_axis=0, concat_axis=0, tiled=True)  11.5 us
    all_to_all x1, starting transfers between devices, sent_to_all(): return lax.all_to_all(copies, axis, split_axis=0, concat_axis=0, tiled=True)  9.85 us
    dot_general x1, matrix products, local(): jnp.dot(grads, down_weight.T, preferred_element_type=jnp.float32)  8.16 us
  transfers between devices with their start and end apart: 9, of which 8 were waited for; matrix products, arithmetic and copies ran while one was open for 17% of the time, Pallas kernels for 0%

commit v1 on v0

v1 whole, which is shorter than its diff:
```python
import functools

import jax
import jax.numpy as jnp
from jax import lax
from jax.experimental import pallas as pl
from jax.experimental.pallas import tpu as pltpu
from jax.sharding import PartitionSpec as P

MESH = pl.DeviceIdType.MESH
bf16, f32 = jnp.bfloat16, jnp.float32

epsilon = 1e-05
gelu_c = 0.7978845608028654
gelu_a = 0.044715

N_REP, N_TP = 32, 8
NX, NY, NZ = 4, 4, 8
IMG, CAP, SLAB, D, FFL = 16, 32, 6, 1280, 640
SROWS = SLAB * CAP
HALF = SROWS // 2
ROWS = SROWS * N_TP
MSG = 1024
TAIL = D - MSG
VMEM_BYTES = 62 * 1024 * 1024


def wrap(value, n):
    return lax.rem(value + n, n)


def place():
    rep, tp = lax.axis_index("rep"), lax.axis_index("tp")
    z, y = rep // NY, lax.rem(rep, NY)
    x, core = tp // 2, lax.rem(tp, 2)
    return rep, tp, z, y, x, core


def greet(peers):
    barrier = pltpu.get_barrier_semaphore()
    for peer in peers:
        pl.semaphore_signal(barrier, inc=1, device_id=peer, device_id_type=MESH)
    return lambda: pl.semaphore_wait(barrier, len(peers))


def remote(src, dst, sems, index, device):
    return pltpu.make_async_remote_copy(
        src_ref=src,
        dst_ref=dst,
        send_sem=sems[0].at[index],
        recv_sem=sems[1].at[index],
        device_id=device,
        device_id_type=MESH,
    )


def iota(shape, dim):
    return lax.broadcasted_iota(jnp.int32, shape, dim)


def pick(mask):
    return jnp.where(mask, 1.0, 0.0).astype(bf16)


def dot(a, b):
    return jnp.dot(a, b, preferred_element_type=f32)


def pack(img_ref, rank_ref, slot_ref, packed):
    rows, cols = N_REP * 8, SLAB * IMG
    row, col = iota((rows, cols), 0), iota((rows, cols), 1)
    owner = (row // 8) == rank_ref[...]
    part, patch = lax.rem(row, 8), col // IMG
    main = pick(owner & (part == patch))
    tail = img_ref[:, MSG:]
    for j in range(3):
        q = pick(owner & (part >= SLAB) & (patch == 3 * (part - SLAB) + j))
        block = dot(main, img_ref[:, j * TAIL : (j + 1) * TAIL]) + dot(q, tail)
        packed[:, j * TAIL : (j + 1) * TAIL] = block.astype(bf16)
    mark = jnp.where(owner & (part == SLAB) & (patch == 0), slot_ref[...] + 1, 0)
    mark = jnp.sum(mark.astype(f32), axis=1, keepdims=True)
    block = dot(main, img_ref[:, 3 * TAIL : MSG]) + mark
    packed[:, 3 * TAIL :] = block.astype(bf16)


def unpack(inbound, store):
    rows = N_REP * 8
    row, col = iota((rows, rows), 0), iota((rows, rows), 1)
    marks = jnp.where(
        (lax.rem(row, 8) == SLAB) & (row // 8 == col // 8), inbound[:, 3 * TAIL :], 0.0
    ).astype(bf16)
    ones = jnp.ones((SROWS, rows), bf16)
    slots = dot(ones, marks)
    row, col = iota((SROWS, rows), 0), iota((SROWS, rows), 1)
    here = slots == (lax.rem(row, CAP) + 1).astype(f32)
    part, patch = lax.rem(col, 8), row // CAP
    main = pick(here & (part == patch))
    tail = jnp.zeros((SROWS, TAIL), f32)
    for j in range(3):
        q = pick(here & (part >= SLAB) & (patch == 3 * (part - SLAB) + j))
        tail = tail + dot(q, inbound[:, j * TAIL : (j + 1) * TAIL])
    store(dot(main, inbound[...]).astype(bf16), tail.astype(bf16))


def dispatch_kernel(img_ref, rank_ref, slot_ref, out, packed, inbound, ds, dr, xs, xr, cs, cr, ls):
    rep, tp, z, y, x, core = place()
    right = (rep, wrap(x + 1, NX) * 2 + core)
    left = (rep, wrap(x - 1, NX) * 2 + core)
    partner = (rep, x * 2 + 1 - core)
    others = [(wrap(rep + i, N_REP), tp) for i in range(1, N_REP)]
    entered = greet(others + [right, left, partner])
    pack(img_ref, rank_ref, slot_ref, packed)
    entered()

    def message(i, peer):
        return remote(
            packed.at[pl.ds(peer * 8, 8)], inbound.at[pl.ds(rep * 8, 8)], (ds, dr), i, (peer, tp)
        )

    def send(i, _):
        message(i, wrap(rep + i, N_REP)).start()
        return 0

    lax.fori_loop(1, N_REP, send, 0)
    own = pltpu.make_async_copy(packed.at[pl.ds(rep * 8, 8)], inbound.at[pl.ds(rep * 8, 8)], ls)
    own.start()
    own.wait()

    def finish(i, _):
        message(i, wrap(rep + i, N_REP)).wait()
        return 0

    lax.fori_loop(1, N_REP, finish, 0)

    def rows(slab, half):
        return out.at[pl.ds(pl.multiple_of(slab * SROWS + half * HALF, HALF), HALF)]

    def keep(main, tail):
        at = pl.ds(pl.multiple_of(tp * SROWS, SROWS), SROWS)
        out[at, :MSG] = main
        out[at, MSG:] = tail

    unpack(inbound, keep)

    def across(i, slab, half, peer):
        return remote(rows(slab, half), rows(slab, half), (xs, xr), i, peer)

    def beside(i, slab, half):
        return remote(rows(slab, half), rows(slab, half), (cs, cr), i, partner)

    lslab, rslab = wrap(x - 1, NX) * 2 + core, wrap(x + 1, NX) * 2 + core
    oslab = wrap(x + 2, NX) * 2 + core
    sent = []

    def go(copy):
        copy.start()
        sent.append(copy)

    go(across(0, tp, 0, right))
    go(across(1, tp, 1, left))
    go(across(2, tp, 1, right))
    go(across(3, tp, 0, left))
    go(beside(0, tp, 0))
    go(beside(1, tp, 1))
    across(0, lslab, 0, right).wait_recv()
    go(across(4, lslab, 0, right))
    go(beside(2, lslab, 0))
    across(1, rslab, 1, left).wait_recv()
    go(across(5, rslab, 1, left))
    go(beside(3, rslab, 1))
    across(2, lslab, 1, right).wait_recv()
    go(beside(4, lslab, 1))
    across(3, rslab, 0, left).wait_recv()
    go(beside(5, rslab, 0))
    across(4, oslab, 0, right).wait_recv()
    go(beside(6, oslab, 0))
    across(5, oslab, 1, left).wait_recv()
    go(beside(7, oslab, 1))
    flip = 1 - 2 * core
    for i, (slab, half) in enumerate(
        [(tp, 0), (tp, 1), (lslab, 0), (rslab, 1), (lslab, 1), (rslab, 0), (oslab, 0), (oslab, 1)]
    ):
        beside(i, slab + flip, half).wait_recv()
    for copy in sent:
        copy.wait_send()


def dispatch(images, dest_rank, dest_slot):
    flat = images.transpose(1, 0, 2).reshape(SLAB * IMG, D)
    rank = jnp.tile(dest_rank, SLAB)[None, :]
    slot = jnp.tile(dest_slot, SLAB)[None, :]
    dma = pltpu.SemaphoreType.DMA
    return pl.pallas_call(
        dispatch_kernel,
        out_shape=jax.ShapeDtypeStruct((ROWS, D), bf16),
        in_specs=[pl.BlockSpec(memory_space=pltpu.VMEM)] * 3,
        out_specs=pl.BlockSpec(memory_space=pltpu.VMEM),
        scratch_shapes=[
            pltpu.VMEM((N_REP * 8, MSG), bf16),
            pltpu.VMEM((N_REP * 8, MSG), bf16),
            dma((N_REP,)),
            dma((N_REP,)),
            dma((6,)),
            dma((6,)),
            dma((8,)),
            dma((8,)),
            dma,
        ],
        compiler_params=pltpu.CompilerParams(
            collective_id=0, has_side_effects=True, vmem_limit_bytes=VMEM_BYTES
        ),
        name="dispatch",
    )(flat, rank, slot)


def add(*terms):
    total = terms[0].astype(f32)
    for term in terms[1:]:
        total = total + term.astype(f32)
    return total


def reduce_kernel(
    part, up, down, gain, gn_out, up_out, down_out, gain_out,
    pr, q, tfar, tnear,
    ua, uacc, uin, ufar, uw, uzi, uzs,
    dzi, dzs, dw, dfar, dacc, din,
    gbuf, ss, rs,
):
    rep, tp, z, y, x, core = place()
    me = (rep, tp)
    partner = (rep, x * 2 + 1 - core)
    xr, xl = (rep, wrap(x + 1, NX) * 2 + core), (rep, wrap(x - 1, NX) * 2 + core)

    def at_y(k):
        return (z * NY + wrap(y + k, NY), tp)

    def at_z(k):
        return (wrap(z + k, NZ) * NY + y, tp)

    tps = [(rep, wrap(tp + i, N_TP)) for i in range(1, N_TP)]
    ys = [at_y(i) for i in range(1, NY)]
    zs = [at_z(i) for i in range(1, NZ)]
    entered = greet(tps + ys + zs)
    sent = []
    waits = {}
    count = [0]

    def go(key, src, dst, device):
        copy = remote(src, dst, (ss, rs), count[0], device)
        count[0] += 1
        copy.start()
        sent.append(copy)
        waits[key] = copy

    def got(key):
        waits[key].wait_recv()

    A, B = pl.ds(0, HALF), pl.ds(HALF, HALF)
    entered()

    def slab(k, half):
        start = pl.multiple_of(k * SROWS + half * HALF, HALF)
        return pl.ds(start, HALF)

    order = [wrap(x + 2, NX), wrap(x + 1, NX), wrap(x - 1, NX), x]
    for i, to in enumerate(order):
        for h in range(2):
            go(("pair", i, h), part.at[slab(to * 2 + 1 - core, h)], pr.at[i, h], partner)
    ylo, yhi = pl.ds(0, NZ // 2), pl.ds(NZ // 2, NZ // 2)
    yfar, yright, yleft = wrap(y + 2, NY), wrap(y + 1, NY), wrap(y - 1, NY)
    go("u0r", up.at[ylo, yfar], ufar.at[0], at_y(1))
    go("u0l", up.at[yhi, yfar], ufar.at[1], at_y(-1))
    go("u1r", up.at[yhi, yright], uin.at[0, yhi], at_y(1))
    go("u1l", up.at[ylo, yleft], uin.at[1, ylo], at_y(-1))
    dfirst = wrap(z + 4, NZ)
    go("d0r", down.at[dfirst, pl.ds(0, 2)], dzi.at[0, 0, pl.ds(0, 2)], at_z(1))
    go("d0l", down.at[dfirst, pl.ds(2, 2)], dzi.at[1, 0, pl.ds(2, 2)], at_z(-1))
    gbuf[0, 0] = gain[...]
    for i in range(1, N_TP):
        go(("g0", i), gbuf.at[0, 0], gbuf.at[0, i], tps[i - 1])

    def pair_sum(i, to):
        for h in range(2):
            got(("pair", i, h))
            q[i, h] = add(part[slab(to * 2 + core, h), :], pr[i, h]).astype(bf16)

    pair_sum(0, order[0])
    go("t0r", q.at[0, 0], tfar.at[0], xr)
    go("t0l", q.at[0, 1], tfar.at[1], xl)
    pair_sum(1, order[1])
    go("t1r", q.at[1, 1], tnear.at[0, 1], xr)
    pair_sum(2, order[2])
    go("t1l", q.at[2, 0], tnear.at[1, 0], xl)

    def down_step(k):
        for side, sign in ((0, 1), (1, -1)):
            name = "rl"[side]
            got(f"d{k - 1}{name}")
            to = wrap(z + sign * (4 - k), NZ)
            if k == 1:
                near, other = (pl.ds(0, 2), pl.ds(2, 2)) if side == 0 else (pl.ds(2, 2), pl.ds(0, 2))
                dzs[side, 0, near] = add(down[to, near], dzi[side, 0, near]).astype(bf16)
                dzs[side, 0, other] = down[to, other]
            else:
                dzs[side, k - 1] = add(down[to], dzi[side, k - 1]).astype(bf16)
            go(f"d{k}{name}", dzs.at[side, k - 1], dzi.at[side, k], at_z(sign))

    down_step(1)
    got("u0r")
    uacc[0] = add(up[ylo, yright], ufar[0]).astype(bf16)
    go("u2r", uacc.at[0], uin.at[0, ylo], at_y(1))
    got("u0l")
    uacc[1] = add(up[yhi, yleft], ufar[1]).astype(bf16)
    go("u2l", uacc.at[1], uin.at[1, yhi], at_y(-1))
    got("t0r")
    q[1, 0] = add(q[1, 0], tfar[0]).astype(bf16)
    go("t2r", q.at[1, 0], tnear.at[0, 0], xr)
    got("t0l")
    q[2, 1] = add(q[2, 1], tfar[1]).astype(bf16)
    go("t2l", q.at[2, 1], tnear.at[1, 1], xl)
    for i in range(1, N_TP):
        got(("g0", i))
    gbuf[1, 0] = jnp.sum(gbuf[0], axis=0)
    for i in range(1, NY):
        go(("g1", i), gbuf.at[1, 0], gbuf.at[1, i], ys[i - 1])
    down_step(2)
    for key in ("u1r", "u1l", "u2r", "u2l"):
        got(key)
    uw[...] = add(up[:, y], uin[0], uin[1]).astype(bf16)
    lo, hi = pl.ds(0, 24), pl.ds(24, 16)
    ufirst = wrap(z + 4, NZ)
    go("z0r", uw.at[ufirst, lo], uzi.at[0, 0, lo], at_z(1))
    go("z0l", uw.at[ufirst, hi], uzi.at[1, 0, hi], at_z(-1))
    down_step(3)

    def up_step(k):
        for side, sign in ((0, 1), (1, -1)):
            name = "rl"[side]
            got(f"z{k - 1}{name}")
            to = wrap(z + sign * (4 - k), NZ)
            if k == 1:
                near, other = (lo, hi) if side == 0 else (hi, lo)
                uzs[side, 0, near] = add(uw[to, near], uzi[side, 0, near]).astype(bf16)
                uzs[side, 0, other] = uw[to, other]
            else:
                uzs[side, k - 1] = add(uw[to], uzi[side, k - 1]).astype(bf16)
            go(f"z{k}{name}", uzs.at[side, k - 1], uzi.at[side, k], at_z(sign))

    up_step(1)
    for i in range(1, NY):
        got(("g1", i))
    gbuf[2, 0] = gbuf[1, 0] + gbuf[1, 1] + gbuf[1, 2] + gbuf[1, 3]
    for i in range(1, NZ):
        go(("g2", i), gbuf.at[2, 0], gbuf.at[2, i], zs[i - 1])
    up_step(2)
    got("d3r")
    got("d3l")
    dw[...] = add(down[z], dzi[0, 3], dzi[1, 3]).astype(bf16)
    go("e0r", dw.at[yfar, lo], dfar.at[0, lo], at_y(1))
    go("e0l", dw.at[yfar, hi], dfar.at[1, hi], at_y(-1))
    go("e1r", dw.at[yright, hi], din.at[0, hi], at_y(1))
    go("e1l", dw.at[yleft, lo], din.at[1, lo], at_y(-1))
    up_step(3)
    pair_sum(3, order[3])
    for key in ("t1r", "t1l", "t2r", "t2l"):
        got(key)
    for h in range(2):
        gn_out[pl.ds(h * HALF, HALF), :] = add(q[3, h], tnear[0, h], tnear[1, h])
    got("e0r")
    dacc[lo] = add(dw[yright, lo], dfar[0, lo]).astype(bf16)
    go("e2r", dacc.at[lo], din.at[0, lo], at_y(1))
    got("e0l")
    dacc[hi] = add(dw[yleft, hi], dfar[1, hi]).astype(bf16)
    go("e2l", dacc.at[hi], din.at[1, hi], at_y(-1))
    got("z3r")
    got("z3l")
    up_out[...] = add(uw[z], uzi[0, 3], uzi[1, 3])
    for key in ("e1r", "e1l", "e2r", "e2l"):
        got(key)
    down_out[...] = add(dw[y], din[0], din[1])
    for i in range(1, NZ):
        got(("g2", i))
    gain_out[...] = jnp.sum(gbuf[2], axis=0)
    for copy in sent:
        copy.wait_send()


N_COPIES = 8 + 4 + 2 + 7 + 2 + 2 + 2 + 2 + 2 + 3 + 2 + 2 + 2 + 2 + 7 + 2 + 4 + 2 + 2 + 8


def reduce_all(part, up, down, gain):
    dma = pltpu.SemaphoreType.DMA
    shape = jax.ShapeDtypeStruct
    vm = pltpu.VMEM
    return pl.pallas_call(
        reduce_kernel,
        out_shape=[shape((SROWS, D), f32), shape((40, FFL), f32), shape((40, FFL), f32), shape((1, D), f32)],
        in_specs=[pl.BlockSpec(memory_space=pltpu.VMEM)] * 4,
        out_specs=[pl.BlockSpec(memory_space=pltpu.VMEM)] * 4,
        scratch_shapes=[
            vm((4, 2, HALF, D), bf16), vm((4, 2, HALF, D), bf16), vm((2, HALF, D), bf16), vm((2, 2, HALF, D), bf16),
            vm((8, 128), f32), vm((2, 4, 40, FFL), bf16), vm((2, NZ, 40, FFL), bf16), vm((2, 4, 40, FFL), bf16),
            vm((NZ, 40, FFL), bf16), vm((2, 4, 40, FFL), bf16), vm((2, 3, 40, FFL), bf16),
            vm((2, 4, NY, 40, FFL), bf16), vm((2, 3, NY, 40, FFL), bf16), vm((NY, 40, FFL), bf16),
            vm((2, 40, FFL), bf16), vm((40, FFL), bf16), vm((2, 40, FFL), bf16),
            vm((3, 8, 1, D), f32),
            dma((N_COPIES,)), dma((N_COPIES,)),
        ],
        compiler_params=pltpu.CompilerParams(
            collective_id=1, has_side_effects=True, vmem_limit_bytes=VMEM_BYTES
        ),
        name="reduce_all",
    )(part, up.reshape(NZ, NY, 40, FFL), down.reshape(NZ, NY, 40, FFL), gain)


def gelu_parts(preact):
    inner = jnp.tanh(gelu_c * (preact + gelu_a * preact**3))
    value = 0.5 * preact * (1.0 + inner)
    slope = 0.5 * (1.0 + inner) + 0.5 * preact * (1.0 - inner * inner) * gelu_c * (
        1.0 + 3.0 * gelu_a * preact * preact
    )
    return value, slope


def normalise(values):
    values = values.astype(f32)
    mean_v = jnp.mean(values, axis=1, keepdims=True)
    var_v = jnp.mean((values - mean_v) ** 2, axis=1, keepdims=True)
    inv_std = 1.0 / jnp.sqrt(var_v + epsilon)
    return (values - mean_v) * inv_std, inv_std


def local(image_grads, dest_rank, dest_slot, saved_inputs, up_weight, down_weight, norm_gain):
    grads = dispatch(image_grads, dest_rank, dest_slot)
    values = saved_inputs.transpose(1, 0, 2).reshape(ROWS, D)
    centred, _ = normalise(values)
    normed = (centred * norm_gain[None, :]).astype(bf16)
    preact = dot(normed, up_weight)
    value, slope = gelu_parts(preact)
    hidden = value.astype(bf16)
    grad_hidden = dot(grads, down_weight.T)
    grad_pre = (grad_hidden * slope).astype(bf16)
    down_local = dot(grads.T, hidden)
    up_local = dot(normed.T, grad_pre)
    partial_normed = dot(grad_pre, up_weight.T).astype(bf16)
    gain_local = jnp.sum(up_local * up_weight.astype(f32), axis=1) / norm_gain
    slab_normed, up_grads, down_grads, gain_grads = reduce_all(
        partial_normed, up_local.astype(bf16), down_local.astype(bf16), gain_local[None, :]
    )
    start = lax.axis_index("tp") * SROWS
    own = lax.dynamic_slice_in_dim(grads, start, SROWS, 0).astype(f32)
    start = lax.axis_index("tp") * SLAB
    own_x = lax.dynamic_slice_in_dim(saved_inputs, start, SLAB, 1)
    centred, inv_std = normalise(own_x.transpose(1, 0, 2).reshape(SROWS, D))
    scaled = slab_normed * norm_gain[None, :]
    first = jnp.mean(scaled, axis=1, keepdims=True)
    second = jnp.mean(scaled * centred, axis=1, keepdims=True)
    result = (own + inv_std * (scaled - first - centred * second)).astype(bf16)
    input_grads = result.reshape(SLAB, CAP, D).transpose(1, 0, 2)
    return (input_grads, up_grads, down_grads.T, gain_grads[0])


def solution(mesh):
    return jax.shard_map(
        local,
        mesh=mesh,
        in_specs=(
            P("rep", "tp", None),
            P("rep"),
            P("rep"),
            P("rep", None, None),
            P(None, "tp"),
            P("tp", None),
            P(),
        ),
        out_specs=(P("rep", "tp", None), P("rep", "tp"), P("tp", "rep"), P()),
        check_vma=False,
    )
```

time: 319 us -> 143 us (0.45)
  waiting for transfers between devices: 206 us -> 0 us
  Pallas kernels: 0 us -> 86.5 us
  starting transfers between devices: 25.9 us -> 0 us
  between operations: 14.3 us -> 0.78 us
  matrix products: 32.8 us -> 25 us
  local copies, waits for them, and re-layouts: 13.3 us -> 6.35 us
    pallas_call x0 -> x2, Pallas kernels: none -> 86.5 us  [the longest x1 44.6 us: dispatch(): pl.pallas_call(dispatch_kernel, out_shape=jax.ShapeDtypeStruct((ROWS, D),...]
    psum x1 -> x0, waiting for transfers between devices: 74.8 us -> none  [local(): lax.psum(partial_normed.astype(jnp.bfloat16), 'tp').astype(jnp.float32)]
    reduce_scatter x2 -> x0, waiting for transfers between devices: 52.3 us -> none  [scatter_axes(): nearer = lax.psum_scatter(value, axes[0], scatter_dimension=dim, tiled=True)]
    unnamed x8 -> x0, waiting for transfers between devices: 40.7 us -> none
    all_to_all x3 -> x0, waiting for transfers between devices: 25.7 us -> none  [the longest x1 18.5 us: local(): lax.all_to_all(packed, REP, split_axis=0, concat_axis=0, tiled=True)]
    all_to_all x3 -> x0, starting transfers between devices: 25.2 us -> none  [the longest x1 11.5 us: local(): lax.all_to_all(slot_sent, REP, split_axis=0, concat_axis=0, tiled=True)]
    all_gather x1 -> x0, waiting for transfers between devices: 12.3 us -> none  [local(): lax.all_gather(compact(inbound, slot_recv, capacity), 'tp', axis=1, tiled...]
    dot_general x7 -> x5, matrix products: 32.8 us -> 25 us  [dot(): return jnp.dot(a, b, preferred_element_type=f32)]
  transfers between devices with their start and end apart: 9 -> 0, of which waited for: 8 -> 0; matrix products, arithmetic and copies ran while one was open for 17% -> 0% of each run, Pallas kernels for 0% -> 0%
where the time goes in v1:
time: 143 us
  Pallas kernels  86.5 us (60%)
  matrix products  25 us (17%)
  other arithmetic  24 us (17%)
  local copies, waits for them, and re-layouts  6.35 us (4%)
    pallas_call x1, Pallas kernels, dispatch(): pl.pallas_call(dispatch_kernel, out_shape=jax.ShapeDtypeStruct((ROWS, D),...  44.6 us
    pallas_call x1, Pallas kernels, reduce_all(): pl.pallas_call(reduce_kernel, out_shape=[shape((SROWS, D), f32), shape((4...  41.9 us
    dot_general x5, matrix products, dot(): return jnp.dot(a, b, preferred_element_type=f32)  25 us
    reduce_sum x2, other arithmetic, normalise(): var_v = jnp.mean((values - mean_v) ** 2, axis=1, keepdims=True)  6.69 us
    reduce_sum x2, other arithmetic, normalise(): mean_v = jnp.mean(values, axis=1, keepdims=True)  4.89 us
    convert_element_type x1, other arithmetic, local(): normed = (centred * norm_gain[None, :]).astype(bf16)  4.33 us

profile of v1, /device:TPU:2, one launch (start us, length us, event | category | flops | bytes accessed | tf_op | source)
XLA Modules:
  0.0 142.6 jit_solution(5022685475578903072)
XLA Ops:
  0.6 0.0 copy-start
  0.7 0.8 tile.4
  1.4 0.6 broadcast_in_dim_tile.6.rank_ref
  2.0 0.7 tile.5
  2.7 0.6 broadcast_in_dim_tile.7.slot_ref
  3.3 1.7 %fusion.19 = f32[6,32]{0,1:T(8,128)S(1)} fusion(bf16[32,48,1280]{2,1,0:T(8,128)(2,1)} %param.10, s32[]{:T(128)S(6)} %select_n.7), kind=kLoop, calls=%fused_computation.34 | loop fusion | flops 491328 | bytes 492292 | tf_op jit(solution)/shard_map/reduce_sum | solution.py:428
  4.9 0.1 copy.19
  5.0 0.1 div.36
  5.1 0.1 copy.20
  5.2 1.8 %multiply_reduce_fusion.1 = f32[6,32]{0,1:T(8,128)S(1)} fusion(f32[6,32]{0,1:T(8,128)S(1)} %copy.20, bf16[32,48,1280]{2,1,0:T(8,128)(2,1)} %param.10, s32[]{:T(128)S(6)} %select_n.7), kind=kLoop, calls=%fused_computation.28 | loop fusion | flops 982848 | bytes 493060 | tf_op jit(solution)/shard_map/reduce_sum | solution.py:429
  6.9 0.1 copy.21
  7.0 0.1 sqrt.11
  7.1 3.2 %bitcast_reduce_fusion = f32[48,32]{1,0:T(8,128)S(1)} fusion(bf16[32,48,1280]{2,1,0:T(8,128)(2,1)} %param.10), kind=kLoop, calls=%fused_computation.4 | loop fusion | flops 3930624 | bytes 3938304 | tf_op jit(solution)/shard_map/reduce_sum | solution.py:428
  10.4 0.1 div.32
  10.4 4.9 %fusion.4 = f32[48,32]{1,0:T(8,128)S(1)} fusion(f32[48,32]{1,0:T(8,128)S(1)} %broadcast_multiply_fusion, bf16[32,48,1280]{2,1,0:T(8,128)(2,1)} %param.10), kind=kLoop, calls=%fused_computation.7 | loop fusion | flops 7862784 | bytes 3944448 | tf_op jit(solution)/shard_map/reduce_sum | solution.py:429
  15.4 0.0 copy-start.5
  15.4 0.1 sqrt.13
  15.4 0.0 copy-start.1
  15.4 1.6 %convert_bitcast_fusion = f32[6,32,1280]{2,0,1:T(8,128)S(1)} fusion(bf16[32,48,1280]{2,1,0:T(8,128)(2,1)} %param.10, s32[]{:T(128)S(6)} %select_n.7), kind=kLoop, calls=%fused_computation.27 | loop fusion | flops 245760 | bytes 1474564 | tf_op jit(solution)/shard_map/convert_element_type | solution.py:427
  17.1 0.3 copy.23
  17.4 0.0 copy-start.2
  17.4 0.9 copy-done.2
  18.4 1.1 fusion.18
  19.5 0.0 copy-done.5
  19.5 0.0 copy-done.1
  19.5 4.3 %fusion.2 = bf16[1536,1280]{1,0:T(8,128)(2,1)} fusion(f32[1280]{0:T(1024)S(1)} %copy-done.5, f32[1536]{0:T(1024)S(1)} %sqrt.13, f32[1536]{0:T(1024)S(1)} %div.32, bf16[32,48,1280]{2,1,0:T(8,128)(2,1)S(1)} %copy-done.1), kind=kLoop, calls=%fused_computation.3 | loop fusion | flops 9830400 | bytes 7881728 | tf_op jit(solution)/shard_map/convert_element_type | solution.py:438
  23.8 44.6 %dispatch.1 = bf16[1536,1280]{1,0:T(8,128)(2,1)} custom-call(bf16[96,1280]{1,0:T(8,128)(2,1)} %bitcast.49, s32[1,96]{1,0:T(1,128)} %broadcast_in_dim_tile.6.rank_ref, s32[1,96]{1,0:T(1,128)} %broadcast_in_dim_tile.7.slot_ref), custom_call_target="tpu_custom_call" | custom-call | tf_op jit(solution)/shard_map/dispatch/pallas_call | solution.py:193
  68.5 0.0 copy-start.3
  68.5 6.0 %fusion.24 = f32[1536,640]{1,0:T(8,128)S(1)} fusion(bf16[1536,1280]{1,0:T(8,128)(2,1)} %fusion.2, bf16[1280,640]{1,0:T(8,128)(2,1)} %param.11), kind=kOutput, calls=%fused_computation.45 | convolution fusion | flops 2516582400 | bytes 9502720 | tf_op jit(solution)/shard_map/dot_general | solution.py:66
  74.5 0.0 copy-done.3
  74.5 4.8 %convolution_convert_fusion.1 = bf16[1280,640]{1,0:T(8,128)(2,1)} fusion(bf16[1536,1280]{1,0:T(8,128)(2,1)S(1)} %copy-done.3, f32[1536,640]{1,0:T(8,128)S(1)} %fusion.24), kind=kOutput, calls=%fused_computation.22 | convolution fusion | flops 2526248960 | bytes 9502720 | tf_op jit(solution)/shard_map/dot_general | solution.py:66
  79.3 0.0 copy-done
  79.3 0.0 copy-start.4
  79.3 0.0 copy-start.9
  79.3 4.7 %fusion.13 = bf16[1536,640]{1,0:T(8,128)(2,1)S(1)} fusion(f32[1536,640]{1,0:T(8,128)S(1)} %fusion.24, bf16[1536,1280]{1,0:T(8,128)(2,1)S(1)} %copy-done.3, bf16[640,1280]{1,0:T(8,128)(2,1)S(1)} %copy-done), kind=kOutput, calls=%fused_computation.19 | convolution fusion | flops 2535260160 | bytes 11468800 | tf_op jit(solution)/shard_map/dot_general | solution.py:66
  84.0 0.0 copy-done.4
  84.0 0.0 copy-done.9
  84.1 4.8 %multiply_reduce_fusion = (f32[1280]{0:T(1024)S(1)}, bf16[1280,640]{1,0:T(8,128)(2,1)}) fusion(bf16[1280,640]{1,0:T(8,128)(2,1)S(1)} %copy-done.9, bf16[1536,1280]{1,0:T(8,128)(2,1)S(1)} %copy-done.4, bf16[1536,640]{1,0:T(8,128)(2,1)S(1)} %fusion.13), kind=kOutput, calls=%fused_computation.21 | convolution fusion | flops 2519857920 | bytes 9180160 | tf_op jit(solution)/shard_map/dot_general | solution.py:66
  88.8 0.6 broadcast_in_dim.2.gain
  89.4 4.7 %convolution_convert_fusion.part = bf16[1536,1280]{1,0:T(8,128)(2,1)} fusion(bf16[1536,640]{1,0:T(8,128)(2,1)S(1)} %fusion.13, bf16[1280,640]{1,0:T(8,128)(2,1)S(1)} %copy-done.9), kind=kOutput, calls=%fused_computation.8 | convolution fusion | flops 2518548480 | bytes 7536640 | tf_op jit(solution)/shard_map/dot_general | solution.py:66
  94.2 41.9 %reduce_all.1 = (f32[192,1280]{1,0:T(8,128)}, f32[40,640]{1,0:T(8,128)}, f32[40,640]{1,0:T(8,128)}, f32[1,1280]{1,0:T(1,128)}) custom-call(bf16[1536,1280]{1,0:T(8,128)(2,1)} %convolution_convert_fusion.part, bf16[8,4,40,640]{3,2,1,0:T(8,128)(2,1)} %bitcast.47, bf16[8,4,40,640]{3,2,1,0:T(8,128)(2,1)} %bitcast.46, f32[1,1280]{1,0:T(1,128)} %broadcast_in_dim.2.gain), custom_call_target="tpu_custom_call" | custom-call | tf_op jit(solution)/shard_map/reduce_all/pallas_call | solution.py:396
  136.0 0.0 copy-start.8
  136.1 0.0 copy-start.7
  136.1 0.0 copy-start.6
  136.1 1.8 %multiply_reduce_fusion.3 = (f32[192]{0:T(256)S(1)}, f32[192]{0:T(256)S(1)}) fusion(f32[192,1280]{1,0:T(8,128)} %get-tuple-element.8, f32[1280]{0:T(1024)S(1)} %copy-done.5, f32[192,1280]{1,0:T(8,128)} %fusion.18), kind=kLoop, calls=%fused_computation.33 | loop fusion | flops 982656 | bytes 1972736 | tf_op jit(solution)/shard_map/reduce_sum | solution.py:457
  137.9 2.9 %add_convert_fusion = bf16[192,1280]{1,0:T(8,128)(2,1)} fusion(f32[192,1280]{1,0:T(8,128)} %get-tuple-element.8, f32[192]{0:T(256)S(1)} %get-tuple-element.17, f32[192]{0:T(256)S(1)} %get-tuple-element.18, f32[1280]{0:T(1024)S(1)} %copy-done.5, f32[192]{0:T(256)S(1)} %sqrt.11, bf16[1536,1280]{1,0:T(8,128)(2,1)} %dispatch.1, s32[]{:T(128)S(6)} %select_n.6, ...), kind=kLoop, calls=%fused_computation.31 | loop fusion | flops 2457600 | bytes 2957316 | tf_op jit(solution)/shard_map/convert_element_type | solution.py:459
  140.7 0.0 copy-done.8
  140.7 0.6 reduce.4
  141.3 0.0 copy-done.7
  141.3 0.6 copy.29
  142.0 0.0 copy-done.6
  142.0 0.6 copy.30
  (6 shorter events, 0.0 us)
Async XLA Ops:
  0.6 78.7 %copy-start = (bf16[640,1280]{1,0:T(8,128)(2,1)S(1)}, bf16[640,1280]{1,0:T(8,128)(2,1)}, u32[]{:S(2)}) copy-start(bf16[640,1280]{1,0:T(8,128)(2,1)} %param.12) | copy-start | bytes 4915204
  15.4 4.2 %copy-start.5 = (f32[1280]{0:T(1024)S(1)}, f32[1280]{0:T(1024)}, u32[]{:S(2)}) copy-start(f32[1280]{0:T(1024)} %param.13) | copy-start | bytes 15364
  15.4 4.1 %copy-start.1 = (bf16[32,48,1280]{2,1,0:T(8,128)(2,1)S(1)}, bf16[32,48,1280]{2,1,0:T(8,128)(2,1)}, u32[]{:S(2)}) copy-start(bf16[32,48,1280]{2,1,0:T(8,128)(2,1)} %param.10) | copy-start | bytes 11796484
  17.4 0.9 copy-start.2
  68.5 6.0 %copy-start.3 = (bf16[1536,1280]{1,0:T(8,128)(2,1)S(1)}, bf16[1536,1280]{1,0:T(8,128)(2,1)}, u32[]{:S(2)}) copy-start(bf16[1536,1280]{1,0:T(8,128)(2,1)} %dispatch.1) | copy-start | bytes 11796484
  79.3 4.7 %copy-start.4 = (bf16[1536,1280]{1,0:T(8,128)(2,1)S(1)}, bf16[1536,1280]{1,0:T(8,128)(2,1)}, u32[]{:S(2)}) copy-start(bf16[1536,1280]{1,0:T(8,128)(2,1)} %fusion.2) | copy-start | bytes 11796484
  79.3 4.7 %copy-start.9 = (bf16[1280,640]{1,0:T(8,128)(2,1)S(1)}, bf16[1280,640]{1,0:T(8,128)(2,1)}, u32[]{:S(2)}) copy-start(bf16[1280,640]{1,0:T(8,128)(2,1)} %param.11) | copy-start | bytes 4915204
  136.0 4.7 %copy-start.8 = (f32[1,1280]{1,0:T(1,128)S(1)}, f32[1,1280]{1,0:T(1,128)}, u32[]{:S(2)}) copy-start(f32[1,1280]{1,0:T(1,128)} %get-tuple-element.11) | copy-start | bytes 15364
  136.1 5.3 %copy-start.7 = (f32[40,640]{1,0:T(8,128)S(1)}, f32[40,640]{1,0:T(8,128)}, u32[]{:S(2)}) copy-start(f32[40,640]{1,0:T(8,128)} %get-tuple-element.24) | copy-start | bytes 307204
  136.1 5.9 %copy-start.6 = (f32[40,640]{1,0:T(8,128)S(1)}, f32[40,640]{1,0:T(8,128)}, u32[]{:S(2)}) copy-start(f32[40,640]{1,0:T(8,128)} %get-tuple-element.10) | copy-start | bytes 307204
